TPU v7x, 32 devices: a whole 2x2x4 slice. The times are simulated.
32 devices in a mesh: src: 4 (over y, core), help: 8 (over z, x).
Axes of the slice: x: 2, y: 2, z: 4, core: 2. Of those that a mesh axis runs over, the one named last changes fastest.
Arguments:
- tiles: int32 [2, 256], P(None, 'src'), may hold values from 0 to 31, as said below
- cell_slot: int32 [2, 32], replicated, may hold values from 0 to 31, as said below
- counts: int32 [32, 2], P(('src', 'help')), may hold values from 128 to 512, as said below
- src_points: bfloat16 [16384, 512], P(('src', 'help')), may hold values from -9 to 9
- tgt_points: bfloat16 [16384, 512], P(('src', 'help')), may hold values from -9 to 9
Outputs:
- source_potential: float32 [16384], P(('src', 'help'))
- target_potential: float32 [16384], P(('src', 'help'))
- transport: float32 [16384, 512], P(('src', 'help'))
Inputs may be any that keep to these rules, and one draw needn't show every extreme that they name: `tiles`: columns come in blocks of 64, block g for group g of 8 cells: a block's source cells have ids g * 8 to g * 8 + 7, its target cells lie in group g or in group g + 1 (group 4 - 1 is followed by group 0); no pair is listed twice, and every source cell and every target cell is named in some column. Each row is a permutation that keeps every cell in its group: cell c is stored at slot cell_slot[side, c], with cell_slot[side, c] // 8 equal to c // 8; slot k is rows k * 512 to k * 512 + 511 of the point arrays. `counts`: rows of a slot at and beyond its count are padding. Both ends of the range occur in each column.
All inputs are finite; a program needn't handle non-finite values.
Results may differ from a plain program's by a relative error of at most 0.004.
Values may be sent and summed in bfloat16 or wider, within the bound.
A program may use at most 192 MiB of HBM per device.

v0:
```python
import math
import jax
import jax.numpy as jnp
from jax import lax
from jax.sharding import PartitionSpec as P

ITERS = 2
EPSILON = 0.2
NEGATIVE = -1e30


def passed_along(array, axis, by):
    count = lax.axis_size(axis)
    return lax.ppermute(array, axis, [(i, (i + by) % count) for i in range(count)])


def combined_all(part, axis, combine):
    gathered = jax.tree.map(lambda a: lax.all_gather(a, axis), part)

    def take(source):
        return jax.tree.map(lambda a: lax.dynamic_index_in_dim(a, source, 0, False), gathered)

    return lax.fori_loop(
        1, lax.axis_size(axis), lambda source, state: combine(state, take(source)), take(0)
    )


def join_parts(first, second):
    highest = jnp.maximum(first[0], second[0])
    return (
        highest,
        first[1] * jnp.exp(first[0] - highest) + second[1] * jnp.exp(second[0] - highest),
    )


def lookup(cell_ids, slot_table):
    matches = cell_ids[:, None] == jnp.arange(slot_table.shape[0], dtype=jnp.int32)[None, :]
    return jnp.sum(jnp.where(matches, slot_table[None, :], 0), axis=1)


def half_norms(points, group_size, cell_rows):
    return 0.5 * jnp.sum(jnp.square(points.astype(jnp.float32)), axis=1).reshape(
        group_size, cell_rows
    )


def shards(tiles, cell_slot, counts, src_points, tgt_points):
    group_size = lax.axis_size("help")
    help_index = lax.axis_index("help")
    src_index = lax.axis_index("src")
    cell_rows = src_points.shape[0]
    width = src_points.shape[1]
    cost_scale = math.sqrt(width)
    source_all, source_counts = (src_points, counts)
    source_cells_held = 1
    own_points, own_counts = (
        lax.all_gather(tgt_points, "help", axis=0, tiled=True),
        lax.all_gather(counts, "help", axis=0, tiled=True),
    )
    next_points, next_counts = passed_along((own_points, own_counts), "src", -1)
    candidates = 2 * group_size
    positions = jnp.arange(cell_rows, dtype=jnp.int32)
    source_live = positions[None, :] < source_counts[:, 0:1]
    target_live = jnp.stack(
        [positions[None, :] < own_counts[:, 1:2], positions[None, :] < next_counts[:, 1:2]], axis=0
    )
    flat_live = target_live.reshape(candidates, cell_rows)
    source_half = half_norms(source_all, source_cells_held, cell_rows)
    target_half = jnp.stack(
        [
            half_norms(own_points, group_size, cell_rows),
            half_norms(next_points, group_size, cell_rows),
        ],
        axis=0,
    )
    flat_half = target_half.reshape(candidates, cell_rows)
    target_points = jnp.concatenate([own_points, next_points], axis=0)
    src_slot = lookup(tiles[0], cell_slot[0])
    tgt_slot = lookup(tiles[1], cell_slot[1])
    src_cells = src_slot % group_size
    tgt_cells = tgt_slot % group_size
    tgt_sides = jnp.where(tgt_slot // group_size == src_index, 0, 1)
    tgt_keys = tgt_sides * group_size + tgt_cells
    key_ids = jnp.arange(candidates, dtype=jnp.int32)
    is_mine = src_cells == help_index
    listed_keys = jnp.any(is_mine[:, None] & (tgt_keys[:, None] == key_ids[None, :]), axis=0)
    inner = lax.dot_general(
        src_points, target_points, (((1,), (1,)), ((), ())), preferred_element_type=jnp.float32
    )
    cost = (source_half[0][:, None] + flat_half.reshape(-1)[None, :] - inner) / cost_scale
    column_live = (flat_live & listed_keys[:, None]).reshape(-1)
    mask = source_live[0][:, None] & column_live[None, :]
    own_live = source_live[0]
    target_table = jnp.zeros((2, group_size, cell_rows), jnp.float32)
    source_table = jnp.zeros((source_cells_held, cell_rows), jnp.float32)
    source_own = jnp.zeros((cell_rows,), jnp.float32)
    target_own = jnp.zeros((cell_rows,), jnp.float32)
    for sweep in range(ITERS):
        row_flat_target = target_table.reshape(candidates, cell_rows)
        row_scores = jnp.where(
            mask, (row_flat_target.reshape(-1)[None, :] - cost) / EPSILON, NEGATIVE
        )
        part_max = jnp.max(row_scores, axis=1)
        part_sum = jnp.sum(jnp.exp(row_scores - part_max[:, None]), axis=1)
        row_source_own = jnp.where(own_live, -EPSILON * (part_max + jnp.log(part_sum)), 0.0)
        row_source_table = row_source_own[None, :]
        source_table = row_source_table
        source_own = row_source_own
        scores = jnp.where(mask, (source_table[0][:, None] - cost) / EPSILON, NEGATIVE)
        peaks = jnp.max(scores, axis=0)
        sums = jnp.sum(jnp.exp(scores - peaks[None, :]), axis=0)
        peaks = peaks.reshape(2, group_size, cell_rows)
        sums = sums.reshape(2, group_size, cell_rows)
        peaks, sums = combined_all((peaks, sums), "help", join_parts)
        carried_max, carried_sum = passed_along((peaks[1], sums[1]), "src", 1)
        joined = join_parts((peaks[0], sums[0]), (carried_max, carried_sum))
        target_group = jnp.where(target_live[0], -EPSILON * (joined[0] + jnp.log(joined[1])), 0.0)
        target_after = passed_along(target_group, "src", -1)
        col_target_table = jnp.stack([target_group, target_after], axis=0)
        col_target_own = target_group[help_index]
        target_table = col_target_table
        target_own = col_target_own
    flat_target = target_table.reshape(candidates, cell_rows)
    exponent = (source_table[0][:, None] + flat_target.reshape(-1)[None, :] - cost) / EPSILON
    weight = jnp.where(mask, jnp.exp(exponent), 0.0).astype(jnp.bfloat16)
    own_numerator = jnp.dot(weight, target_points, preferred_element_type=jnp.float32)
    own_denominator = jnp.sum(weight.astype(jnp.float32), axis=1)
    safe_total = jnp.where(own_live, own_denominator, 1.0)
    transport = jnp.where(own_live[:, None], own_numerator / safe_total[:, None], 0.0)
    return (source_own, target_own, transport)


def solution(mesh):
    in_specs = (
        P(None, "src"),
        P(),
        P(("src", "help"), None),
        P(("src", "help"), None),
        P(("src", "help"), None),
    )
    out_specs = (P(("src", "help")), P(("src", "help")), P(("src", "help"), None))
    return jax.shard_map(shards, mesh=mesh, in_specs=in_specs, out_specs=out_specs, check_vma=False)
```

profile of v0, /device:TPU:1, one launch (start us, length us, event | category | flops | bytes accessed | tf_op | source)
XLA Modules:
  0.0 362.8 jit_solution(11354192799630096327)
XLA Ops:
  7.9 75.9 %all-gather.3.cloned.1.call-done = bf16[4096,512]{1,0:T(8,128)(2,1)} async-done(((bf16[512,512]{1,0:T(8,128)(2,1)}), bf16[4096,512]{1,0:T(8,128)(2,1)}) %all-gather.3.cloned.1.call-update) | async-done | bytes 4194320 | tf_op jit(solution)/shard_map/all_gather | solution.py:57
  83.8 1.9 collective-permute-start.1
  85.7 14.5 %all-gather = s32[8,1,2]{2,1,0:T(1,128)S(1)} all-gather(s32[1,1,2]{2,1,0:T(1,128)} %bitcast.156), channel_id=1, replica_groups=mesh['src'=4,'help'=8] {'help'}, dimensions={0}, use_global_device_ids=true | all-gather | bytes 72 | tf_op jit(solution)/shard_map/all_gather | solution.py:58
  100.3 4.6 %collective-permute-start = (s32[8,2]{0,1:T(2,128)S(1)}, s32[8,2]{0,1:T(2,128)S(1)}, u32[]{:S(2)}, u32[]{:S(2)}) collective-permute-start(s32[8,2]{0,1:T(2,128)S(1)} %bitcast.162), channel_id=1, source_target_pairs={{0,24},{8,0},{16,8},{24,16},{1,25},{9,1},{17,9},{25,17},{2,26},{10... | collective-permute-start | bytes 200 | tf_op jit(solution)/shard_map/ppermute | solution.py:14
  107.3 1.2 multiply_reduce_fusion.2
  108.7 24.6 %collective-permute-done = s32[8,2]{0,1:T(2,128)S(1)} collective-permute-done((s32[8,2]{0,1:T(2,128)S(1)}, s32[8,2]{0,1:T(2,128)S(1)}, u32[]{:S(2)}, u32[]{:S(2)}) %collective-permute-start) | collective-permute-done | bytes 96 | tf_op jit(solution)/shard_map/ppermute | solution.py:14
  133.4 3.1 multiply_reduce_fusion.1
  136.5 4.4 %constant_dynamic-update-slice_fusion.1 = bf16[8192,512]{1,0:T(8,128)(2,1)} fusion(bf16[4096,512]{1,0:T(8,128)(2,1)} %all-gather.3.cloned.1.call-done), kind=kLoop, calls=%fused_computation.82 | loop fusion | bytes 8388608
  140.9 3.1 multiply_reduce_fusion
  144.0 4.4 %constant_dynamic-update-slice_fusion = bf16[8192,512]{1,0:T(8,128)(2,1)} fusion(bf16[8192,512]{1,0:T(8,128)(2,1)} %constant_dynamic-update-slice_fusion.1, bf16[4096,512]{1,0:T(8,128)(2,1)} %collective-permute-done.1), kind=kLoop, calls=%fused_computation.81 | loop fusion | bytes 8388608 | tf_op jit(solution)/shard_map/concatenate | solution.py:77
  148.4 10.4 %fusion.6 = (f32[512]{0:T(512)S(1)}, f32[512,8192]{0,1:T(8,128)S(1)}) fusion(pred[512]{0:T(512)(128)(4,1)S(1)} %iota_compare_fusion.6, pred[8192]{0:T(1024)(128)(4,1)S(1)} %and.81, bf16[8192,512]{1,0:T(8,128)(2,1)} %constant_dynamic-update-slice_fusion, bf16[512,512]{1,0:T(8,128)(2,1)S(1)} %copy-done.2, f32[8192]{0:T(1024)S(1)} %bitcast.153, ...), kind=kOutput, calls=%fused_computation.23 | convolution fusion | flops 4328521216 | bytes 25735680 | tf_op jit(solution)/shard_map/dot_general | solution.py:87
  158.9 7.0 %exponential_reduce_fusion.3 = f32[512]{0:T(512)S(1)} fusion(f32[512,8192]{0,1:T(8,128)S(1)} %get-tuple-element.304, f32[512]{0:T(512)S(1)} %get-tuple-element.303, pred[512]{0:T(512)(128)(4,1)S(1)} %iota_compare_fusion.6, pred[8192]{0:T(1024)(128)(4,1)S(1)} %and.81), kind=kLoop, calls=%fused_computation.22 | loop fusion | flops 25165312 | bytes 16790016 | tf_op jit(solution)/shard_map/reduce_sum | solution.py:104
  166.0 4.8 %fusion.7 = f32[8192]{0:T(1024)S(1)} fusion(f32[512,8192]{0,1:T(8,128)S(1)} %get-tuple-element.304, f32[512]{0:T(512)S(1)} %multiply_select_fusion.1, pred[512]{0:T(512)(128)(4,1)S(1)} %iota_compare_fusion.6, pred[8192]{0:T(1024)(128)(4,1)S(1)} %and.81), kind=kLoop, calls=%fused_computation.24 | loop fusion | flops 20963328 | bytes 16820736 | tf_op jit(solution)/shard_map/reduce_max | solution.py:110
  170.8 6.7 %exponential_reduce_fusion.2 = f32[8192]{0:T(1024)S(1)} fusion(f32[512,8192]{0,1:T(8,128)S(1)} %get-tuple-element.304, f32[8192]{0:T(1024)S(1)} %fusion.7, f32[512]{0:T(512)S(1)} %multiply_select_fusion.1, pred[512]{0:T(512)(128)(4,1)S(1)} %iota_compare_fusion.6, pred[8192]{0:T(1024)(128)(4,1)S(1)} %and.81), kind=kLoop, calls=%fused_computation.21 | loop fusion | flops 25157632 | bytes 16853504 | tf_op jit(solution)/shard_map/reduce_sum | solution.py:111
  177.5 24.8 %all_gather.21 = f32[8,2,8,512]{3,2,1,0:T(8,128)S(1)} all-gather(f32[1,2,8,512]{3,2,1,0:T(8,128)S(1)} %all_gather_reshape.13), channel_id=1, replica_groups=mesh['src'=4,'help'=8] {'help'}, dimensions={0}, use_global_device_ids=true | all-gather | bytes 294912 | tf_op jit(solution)/shard_map/all_gather | solution.py:18
  202.4 24.9 %all_gather.20 = f32[8,2,8,512]{3,2,1,0:T(8,128)S(1)} all-gather(f32[1,2,8,512]{3,2,1,0:T(8,128)S(1)} %all_gather_reshape.12), channel_id=1, replica_groups=mesh['src'=4,'help'=8] {'help'}, dimensions={0}, use_global_device_ids=true | all-gather | bytes 294912 | tf_op jit(solution)/shard_map/all_gather | solution.py:18
  227.7 11.7 %collective-permute-start.2 = (f32[8,512]{1,0:T(8,128)S(1)}, f32[8,512]{1,0:T(8,128)S(1)}, u32[]{:S(2)}, u32[]{:S(2)}) collective-permute-start(f32[8,512]{1,0:T(8,128)S(1)} %slice_bitcast_fusion.7), channel_id=1, source_target_pairs={{0,8},{8,16},{16,24},{24,0},{1,9},{9,17},{17,25},{25,1},{2,10},{10... | collective-permute-start | bytes 49160 | tf_op jit(solution)/shard_map/ppermute | solution.py:14
  239.5 0.8 collective-permute-done.2
  240.7 1.3 collective-permute-start.4
  242.0 2.3 collective-permute-done.4
  244.3 10.3 %fusion.8 = f32[512]{0:T(512)S(1)} fusion(f32[512,8192]{0,1:T(8,128)} %copy-done, f32[8192]{0:T(1024)S(1)} %bitcast.146, pred[512]{0:T(512)(128)(4,1)S(1)} %iota_compare_fusion.6, pred[8192]{0:T(1024)(128)(4,1)S(1)} %and.81), kind=kLoop, calls=%fused_computation.25 | loop fusion | flops 20971008 | bytes 16820736 | tf_op jit(solution)/shard_map/reduce_max | solution.py:103
  254.6 5.6 %exponential_reduce_fusion.1 = f32[512]{0:T(512)S(1)} fusion(f32[512,8192]{0,1:T(8,128)S(1)} %copy-done.1, f32[512]{0:T(512)S(1)} %fusion.8, f32[8192]{0:T(1024)S(1)} %bitcast.147, pred[512]{0:T(512)(128)(4,1)S(1)} %iota_compare_fusion.6, pred[8192]{0:T(1024)(128)(4,1)S(1)} %and.81), kind=kLoop, calls=%fused_computation.20 | loop fusion | flops 25165312 | bytes 16822784 | tf_op jit(solution)/shard_map/reduce_sum | solution.py:104
  260.2 4.8 %fusion.9 = f32[8192]{0:T(1024)S(1)} fusion(f32[512,8192]{0,1:T(8,128)S(1)} %copy-done.1, f32[512]{0:T(512)S(1)} %multiply_select_fusion, pred[512]{0:T(512)(128)(4,1)S(1)} %iota_compare_fusion.6, pred[8192]{0:T(1024)(128)(4,1)S(1)} %and.81), kind=kLoop, calls=%fused_computation.26 | loop fusion | flops 20963328 | bytes 16820736 | tf_op jit(solution)/shard_map/reduce_max | solution.py:110
  265.1 6.7 %exponential_reduce_fusion = f32[8192]{0:T(1024)S(1)} fusion(f32[512,8192]{0,1:T(8,128)S(1)} %copy-done.1, f32[8192]{0:T(1024)S(1)} %fusion.9, f32[512]{0:T(512)S(1)} %multiply_select_fusion, pred[512]{0:T(512)(128)(4,1)S(1)} %iota_compare_fusion.6, pred[8192]{0:T(1024)(128)(4,1)S(1)} %and.81), kind=kLoop, calls=%fused_computation.19 | loop fusion | flops 25157632 | bytes 16853504 | tf_op jit(solution)/shard_map/reduce_sum | solution.py:111
  271.8 25.1 %all_gather.23 = f32[8,2,8,512]{3,2,1,0:T(8,128)S(1)} all-gather(f32[1,2,8,512]{3,2,1,0:T(8,128)S(1)} %all_gather_reshape.15), channel_id=1, replica_groups=mesh['src'=4,'help'=8] {'help'}, dimensions={0}, use_global_device_ids=true | all-gather | bytes 294912 | tf_op jit(solution)/shard_map/all_gather | solution.py:18
  296.9 24.9 %all_gather.22 = f32[8,2,8,512]{3,2,1,0:T(8,128)S(1)} all-gather(f32[1,2,8,512]{3,2,1,0:T(8,128)S(1)} %all_gather_reshape.14), channel_id=1, replica_groups=mesh['src'=4,'help'=8] {'help'}, dimensions={0}, use_global_device_ids=true | all-gather | bytes 294912 | tf_op jit(solution)/shard_map/all_gather | solution.py:18
  322.2 11.8 %collective-permute-start.5 = (f32[8,512]{1,0:T(8,128)S(1)}, f32[8,512]{1,0:T(8,128)S(1)}, u32[]{:S(2)}, u32[]{:S(2)}) collective-permute-start(f32[8,512]{1,0:T(8,128)S(1)} %slice_bitcast_fusion.5), channel_id=1, source_target_pairs={{0,8},{8,16},{16,24},{24,0},{1,9},{9,17},{17,25},{25,1},{2,10},{10... | collective-permute-start | bytes 49160 | tf_op jit(solution)/shard_map/ppermute | solution.py:14
  334.1 0.8 collective-permute-done.5
  335.3 1.4 collective-permute-start.7
  337.3 1.6 collective-permute-done.7
  338.9 8.1 %convert_reduce_fusion = (f32[512]{0:T(512)S(1)}, bf16[512,8192]{0,1:T(8,128)(2,1)S(1)}) fusion(f32[512,8192]{0,1:T(8,128)} %copy-done, f32[8192]{0:T(1024)S(1)} %bitcast.148, f32[512]{0:T(512)S(1)} %multiply_select_fusion, pred[8192]{0:T(1024)(128)(4,1)S(1)} %and.81, pred[512]{0:T(512)(128)(4,1)S(1)} %iota_compare_fusion.6), kind=kLoop, calls=%fused_computation.18 | loop fusion | flops 33553920 | bytes 25211392 | tf_op jit(solution)/shard_map/reduce_sum | solution.py:127
  347.1 8.9 %fusion.10 = f32[512,512]{1,0:T(8,128)} fusion(bf16[512,8192]{0,1:T(8,128)(2,1)S(1)} %get-tuple-element.298, bf16[8192,512]{1,0:T(8,128)(2,1)} %constant_dynamic-update-slice_fusion, f32[512]{0:T(512)S(1)} %broadcast_select_fusion, pred[512]{0:T(512)(128)(4,1)S(1)} %iota_compare_fusion.6), kind=kOutput, calls=%fused_computation.30 | convolution fusion | flops 4295491584 | bytes 17828352 | tf_op jit(solution)/shard_map/dot_general | solution.py:126
  (79 shorter events, 6.4 us)
Async XLA Ops:
  7.2 141.3 %copy-start.2 = (bf16[512,512]{1,0:T(8,128)(2,1)S(1)}, bf16[512,512]{1,0:T(8,128)(2,1)}, u32[]{:S(2)}) copy-start(bf16[512,512]{1,0:T(8,128)(2,1)} %param.12) | copy-start | bytes 1572868
  7.2 76.6 %all-gather.3.cloned.1.call-start = ((), (), s32[]{:S(2)}) async-start(), calls=%async_computation | async-start | bytes 4718592 | tf_op jit(solution)/shard_map/all_gather | solution.py:57
  83.8 57.1 %collective-permute-start.1 = (bf16[4096,512]{1,0:T(8,128)(2,1)}, bf16[4096,512]{1,0:T(8,128)(2,1)}, u32[]{:S(2)}, u32[]{:S(2)}) collective-permute-start(bf16[4096,512]{1,0:T(8,128)(2,1)} %all-gather.3.cloned.1.call-done), channel_id=1, source_target_pairs={{0,24},{8,0},{16,8},{24,16},{1,25},{9,1},{17,9},{25,17},{2,26},{10... | collective-permute-start | bytes 12582920 | tf_op jit(solution)/shard_map/ppermute | solution.py:14
  100.3 33.0 %collective-permute-start = (s32[8,2]{0,1:T(2,128)S(1)}, s32[8,2]{0,1:T(2,128)S(1)}, u32[]{:S(2)}, u32[]{:S(2)}) collective-permute-start(s32[8,2]{0,1:T(2,128)S(1)} %bitcast.162), channel_id=1, source_target_pairs={{0,24},{8,0},{16,8},{24,16},{1,25},{9,1},{17,9},{25,17},{2,26},{10... | collective-permute-start | bytes 200 | tf_op jit(solution)/shard_map/ppermute | solution.py:14
  158.9 11.9 %copy-start = (f32[512,8192]{0,1:T(8,128)}, f32[512,8192]{0,1:T(8,128)S(1)}, u32[]{:S(2)}) copy-start(f32[512,8192]{0,1:T(8,128)S(1)} %get-tuple-element.304) | copy-start | bytes 50331652
  158.9 7.0 %copy-start.4 = (s32[1,2]{1,0:T(1,128)S(1)}, s32[1,2]{1,0:T(1,128)}, u32[]{:S(2)}) copy-start(s32[1,2]{1,0:T(1,128)} %param.11) | copy-start | bytes 28
  227.7 12.6 %collective-permute-start.2 = (f32[8,512]{1,0:T(8,128)S(1)}, f32[8,512]{1,0:T(8,128)S(1)}, u32[]{:S(2)}, u32[]{:S(2)}) collective-permute-start(f32[8,512]{1,0:T(8,128)S(1)} %slice_bitcast_fusion.7), channel_id=1, source_target_pairs={{0,8},{8,16},{16,24},{24,0},{1,9},{9,17},{17,25},{25,1},{2,10},{10... | collective-permute-start | bytes 49160 | tf_op jit(solution)/shard_map/ppermute | solution.py:14
  239.4 1.2 collective-permute-start.3
  240.7 3.6 collective-permute-start.4
  242.0 12.6 %copy-start.1 = (f32[512,8192]{0,1:T(8,128)S(1)}, f32[512,8192]{0,1:T(8,128)}, u32[]{:S(2)}) copy-start(f32[512,8192]{0,1:T(8,128)} %copy-done) | copy-start | bytes 50331652
  260.2 78.7 %copy-start.3 = (f32[512]{0:T(512)}, f32[512]{0:T(512)S(1)}, u32[]{:S(2)}) copy-start(f32[512]{0:T(512)S(1)} %multiply_select_fusion) | copy-start | bytes 6148
  322.2 12.7 %collective-permute-start.5 = (f32[8,512]{1,0:T(8,128)S(1)}, f32[8,512]{1,0:T(8,128)S(1)}, u32[]{:S(2)}, u32[]{:S(2)}) collective-permute-start(f32[8,512]{1,0:T(8,128)S(1)} %slice_bitcast_fusion.5), channel_id=1, source_target_pairs={{0,8},{8,16},{16,24},{24,0},{1,9},{9,17},{17,25},{25,1},{2,10},{10... | collective-permute-start | bytes 49160 | tf_op jit(solution)/shard_map/ppermute | solution.py:14
  334.1 1.2 collective-permute-start.6
  335.3 3.6 collective-permute-start.7
Sparse Core Ops, SparseCore 0:
  10.1 73.6 all-gather.2
where the time goes:
time: 363 us
  blocking collectives  114 us (31%)
  waiting for transfers between devices  107 us (29%)
  other arithmetic  63.1 us (17%)
  starting transfers between devices  32.9 us (9%)
  matrix products  19.3 us (5%)
  between operations  14.4 us (4%)
  local copies, waits for them, and re-layouts  11.2 us (3%)
    all_gather x4, blocking collectives, combined_all(): gathered = jax.tree.map(lambda a: lax.all_gather(a, axis), part)  99.8 us
    all_gather x1, waiting for transfers between devices, shards(): lax.all_gather(tgt_points, 'help', axis=0, tiled=True)  75.9 us
    ppermute x8, starting transfers between devices, passed_along(): lax.ppermute(array, axis, [(i, (i + by) % count) for i in range(count)])  32.8 us
    ppermute x8, waiting for transfers between devices, passed_along(): lax.ppermute(array, axis, [(i, (i + by) % count) for i in range(count)])  30.7 us
    all_gather x1, blocking collectives, shards(): lax.all_gather(counts, 'help', axis=0, tiled=True)  14.5 us
    reduce_sum x2, other arithmetic, shards(): sums = jnp.sum(jnp.exp(scores - peaks[None, :]), axis=0)  13.3 us
    reduce_sum x2, other arithmetic, shards(): part_sum = jnp.sum(jnp.exp(row_scores - part_max[:, None]), axis=1)  12.6 us
    dot_general x1, matrix products, shards(): lax.dot_general(src_points, target_points, (((1,), (1,)), ((), ())), pref...  10.4 us
  transfers between devices with their start and end apart: 9, of which 8 were waited for; matrix products, arithmetic and copies ran while one was open for 3% of the time, Pallas kernels for 0%

commit v1 on v0

--- a/solution.py
+++ b/solution.py
@@ -7,6 +7,18 @@
 ITERS = 2
 EPSILON = 0.2
 NEGATIVE = -1e30
+
+
+def collect(x, axis, dim):
+    ways, here, hop = (lax.axis_size(axis), lax.axis_index(axis), x.shape[dim])
+    line, have = (x, 1)
+    while have < ways:
+        line = jnp.concatenate(
+            [line, lax.ppermute(line, axis, [(d, (d - have) % ways) for d in range(ways)])],
+            axis=dim,
+        )
+        have = 2 * have
+    return jnp.roll(line, here * hop, axis=dim)
 
 
 def passed_along(array, axis, by):
@@ -54,7 +66,7 @@
     source_all, source_counts = (src_points, counts)
     source_cells_held = 1
     own_points, own_counts = (
-        lax.all_gather(tgt_points, "help", axis=0, tiled=True),
+        collect(tgt_points, "help", 0),
         lax.all_gather(counts, "help", axis=0, tiled=True),
     )
     next_points, next_counts = passed_along((own_points, own_counts), "src", -1)

time: 363 us -> 404 us (1.11)
  waiting for transfers between devices: 107 us -> 152 us
  between operations: 14.4 us -> 1.1 us
  starting transfers between devices: 32.9 us -> 40.5 us
  local copies, waits for them, and re-layouts: 11.2 us -> 4.24 us
    ppermute x0 -> x3, waiting for transfers between devices: none -> 123 us  [collect(): lax.ppermute(line, axis, [(d, (d - have) % ways) for d in range(ways)])]
    all_gather x1 -> x0, waiting for transfers between devices: 75.9 us -> none  [shards(): lax.all_gather(tgt_points, 'help', axis=0, tiled=True)]
    ppermute x0 -> x3, starting transfers between devices: none -> 6.5 us  [collect(): lax.ppermute(line, axis, [(d, (d - have) % ways) for d in range(ways)])]
    concatenate x1, local copies, waits for them, and re-layouts: 4.43 us -> 0.14 us  [collect(): return jnp.roll(line, here * hop, axis=dim)]
  transfers between devices with their start and end apart: 9 -> 11, of which waited for: 8 -> 10; matrix products, arithmetic and copies ran while one was open for 3% -> 1% of each run, Pallas kernels for 0% -> 0%
where the time goes in v1:
time: 404 us; the launch traced here: 403 us
  waiting for transfers between devices  152 us (38%)
  blocking collectives  118 us (29%)
  other arithmetic  65.9 us (16%)
  starting transfers between devices  40.5 us (10%)
  matrix products  22.1 us (5%)
  local copies, waits for them, and re-layouts  4.24 us (1%)
    ppermute x3, waiting for transfers between devices, collect(): lax.ppermute(line, axis, [(d, (d - have) % ways) for d in range(ways)])  123 us
    all_gather x4, blocking collectives, combined_all(): gathered = jax.tree.map(lambda a: lax.all_gather(a, axis), part)  100 us
    ppermute x8, starting transfers between devices, passed_along(): lax.ppermute(array, axis, [(i, (i + by) % count) for i in range(count)])  34 us
    ppermute x8, waiting for transfers between devices, passed_along(): lax.ppermute(array, axis, [(i, (i + by) % count) for i in range(count)])  28.1 us
    all_gather x1, blocking collectives, shards(): lax.all_gather(counts, 'help', axis=0, tiled=True)  17.6 us
    reduce_sum x2, other arithmetic, shards(): sums = jnp.sum(jnp.exp(scores - peaks[None, :]), axis=0)  13.4 us
    dot_general x1, matrix products, shards(): lax.dot_general(src_points, target_points, (((1,), (1,)), ((), ())), pref...  13.1 us
    reduce_sum x2, other arithmetic, shards(): part_sum = jnp.sum(jnp.exp(row_scores - part_max[:, None]), axis=1)  12.6 us
  transfers between devices with their start and end apart: 11, of which 10 were waited for; matrix products, arithmetic and copies ran while one was open for 1% of the time, Pallas kernels for 0%

profile of v1, /device:TPU:1, one launch (start us, length us, event | category | flops | bytes accessed | tf_op | source)
XLA Modules:
  0.0 403.3 jit_solution(18038737033744215727)
XLA Ops:
  0.6 5.1 %collective-permute-start.1 = (bf16[512,512]{1,0:T(8,128)(2,1)}, bf16[512,512]{1,0:T(8,128)(2,1)S(1)}, u32[]{:S(2)}, u32[]{:S(2)}) collective-permute-start(bf16[512,512]{1,0:T(8,128)(2,1)} %param.13), channel_id=1, source_target_pairs={{0,7},{1,0},{2,1},{3,2},{4,3},{5,4},{6,5},{7,6},{8,15},{9,8},{10,9... | collective-permute-start | bytes 1572872 | tf_op jit(solution)/shard_map/ppermute | solution.py:17
  5.7 10.9 %collective-permute-done.1 = bf16[512,512]{1,0:T(8,128)(2,1)S(1)} collective-permute-done((bf16[512,512]{1,0:T(8,128)(2,1)}, bf16[512,512]{1,0:T(8,128)(2,1)S(1)}, u32[]{:S(2)}, u32[]{:S(2)}) %collective-permute-start.1) | collective-permute-done | bytes 524320 | tf_op jit(solution)/shard_map/ppermute | solution.py:17
  16.7 1.3 pad_maximum_fusion.8
  18.0 1.2 collective-permute-start.2
  19.2 22.0 %collective-permute-done.2 = bf16[1024,512]{1,0:T(8,128)(2,1)S(1)} collective-permute-done((bf16[1024,512]{1,0:T(8,128)(2,1)S(1)}, bf16[1024,512]{1,0:T(8,128)(2,1)S(1)}, u32[]{:S(2)}, u32[]{:S(2)}) %collective-permute-start.2) | collective-permute-done | bytes 1048608 | tf_op jit(solution)/shard_map/ppermute | solution.py:17
  41.2 2.5 pad_maximum_fusion.3
  46.2 90.5 %collective-permute-done.3 = bf16[2048,512]{1,0:T(8,128)(2,1)S(1)} collective-permute-done((bf16[2048,512]{1,0:T(8,128)(2,1)}, bf16[2048,512]{1,0:T(8,128)(2,1)S(1)}, u32[]{:S(2)}, u32[]{:S(2)}) %collective-permute-start.3) | collective-permute-done | bytes 2097184 | tf_op jit(solution)/shard_map/ppermute | solution.py:17
  137.3 2.7 multiply_reduce_fusion.1
  141.1 17.6 %all-gather = s32[8,1,2]{2,1,0:T(1,128)S(1)} all-gather(s32[1,1,2]{2,1,0:T(1,128)S(1)} %bitcast.154), channel_id=1, replica_groups=mesh['src'=4,'help'=8] {'help'}, dimensions={0}, use_global_device_ids=true | all-gather | bytes 72 | tf_op jit(solution)/shard_map/all_gather | solution.py:70
  158.8 4.9 %collective-permute-start = (s32[8,2]{0,1:T(2,128)S(1)}, s32[8,2]{0,1:T(2,128)S(1)}, u32[]{:S(2)}, u32[]{:S(2)}) collective-permute-start(s32[8,2]{0,1:T(2,128)S(1)} %bitcast.160), channel_id=1, source_target_pairs={{0,24},{8,0},{16,8},{24,16},{1,25},{9,1},{17,9},{25,17},{2,26},{10... | collective-permute-start | bytes 200 | tf_op jit(solution)/shard_map/ppermute | solution.py:26
  164.0 1.2 multiply_reduce_fusion.2
  165.4 23.3 %collective-permute-done = s32[8,2]{0,1:T(2,128)S(1)} collective-permute-done((s32[8,2]{0,1:T(2,128)S(1)}, s32[8,2]{0,1:T(2,128)S(1)}, u32[]{:S(2)}, u32[]{:S(2)}) %collective-permute-start) | collective-permute-done | bytes 96 | tf_op jit(solution)/shard_map/ppermute | solution.py:26
  188.9 3.1 multiply_reduce_fusion
  192.0 13.1 %fusion.6 = (f32[512]{0:T(512)S(1)}, f32[512,8192]{0,1:T(8,128)S(1)}) fusion(pred[512]{0:T(512)(128)(4,1)S(1)} %iota_compare_fusion.6, pred[8192]{0:T(1024)(128)(4,1)S(1)} %and.87, bf16[512,512]{1,0:T(8,128)(2,1)S(1)} %copy-done.5, bf16[4096,512]{1,0:T(8,128)(2,1)} %collective-permute-done.4, bf16[4096,512]{1,0:T(8,128)(2,1)} %get-tuple-element.300, ...), kind=kOutput, calls=%fused_computation.23 | convolution fusion | flops 4345298432 | bytes 25735680 | tf_op jit(solution)/shard_map/dot_general | solution.py:99
  205.2 7.0 %exponential_reduce_fusion.3 = f32[512]{0:T(512)S(1)} fusion(f32[512,8192]{0,1:T(8,128)S(1)} %get-tuple-element.306, f32[512]{0:T(512)S(1)} %get-tuple-element.305, pred[512]{0:T(512)(128)(4,1)S(1)} %iota_compare_fusion.6, pred[8192]{0:T(1024)(128)(4,1)S(1)} %and.87), kind=kLoop, calls=%fused_computation.22 | loop fusion | flops 25165312 | bytes 16790016 | tf_op jit(solution)/shard_map/reduce_sum | solution.py:116
  212.3 4.8 %fusion.7 = f32[8192]{0:T(1024)S(1)} fusion(f32[512,8192]{0,1:T(8,128)S(1)} %get-tuple-element.306, f32[512]{0:T(512)S(1)} %multiply_select_fusion.1, pred[512]{0:T(512)(128)(4,1)S(1)} %iota_compare_fusion.6, pred[8192]{0:T(1024)(128)(4,1)S(1)} %and.87), kind=kLoop, calls=%fused_computation.24 | loop fusion | flops 20963328 | bytes 16820736 | tf_op jit(solution)/shard_map/reduce_max | solution.py:122
  217.1 6.7 %exponential_reduce_fusion.2 = f32[8192]{0:T(1024)S(1)} fusion(f32[512,8192]{0,1:T(8,128)S(1)} %get-tuple-element.306, f32[8192]{0:T(1024)S(1)} %fusion.7, f32[512]{0:T(512)S(1)} %multiply_select_fusion.1, pred[512]{0:T(512)(128)(4,1)S(1)} %iota_compare_fusion.6, pred[8192]{0:T(1024)(128)(4,1)S(1)} %and.87), kind=kLoop, calls=%fused_computation.21 | loop fusion | flops 25157632 | bytes 16853504 | tf_op jit(solution)/shard_map/reduce_sum | solution.py:123
  223.8 25.6 %all_gather.17 = f32[8,2,8,512]{3,2,1,0:T(8,128)S(1)} all-gather(f32[1,2,8,512]{3,2,1,0:T(8,128)S(1)} %all_gather_reshape.13), channel_id=1, replica_groups=mesh['src'=4,'help'=8] {'help'}, dimensions={0}, use_global_device_ids=true | all-gather | bytes 294912 | tf_op jit(solution)/shard_map/all_gather | solution.py:30
  249.5 24.6 %all_gather.16 = f32[8,2,8,512]{3,2,1,0:T(8,128)S(1)} all-gather(f32[1,2,8,512]{3,2,1,0:T(8,128)S(1)} %all_gather_reshape.12), channel_id=1, replica_groups=mesh['src'=4,'help'=8] {'help'}, dimensions={0}, use_global_device_ids=true | all-gather | bytes 294912 | tf_op jit(solution)/shard_map/all_gather | solution.py:30
  274.5 11.8 %collective-permute-start.5 = (f32[8,512]{1,0:T(8,128)S(1)}, f32[8,512]{1,0:T(8,128)S(1)}, u32[]{:S(2)}, u32[]{:S(2)}) collective-permute-start(f32[8,512]{1,0:T(8,128)S(1)} %slice_bitcast_fusion.7), channel_id=1, source_target_pairs={{0,8},{8,16},{16,24},{24,0},{1,9},{9,17},{17,25},{25,1},{2,10},{10... | collective-permute-start | bytes 49160 | tf_op jit(solution)/shard_map/ppermute | solution.py:26
  287.5 2.2 collective-permute-start.7
  289.7 1.6 collective-permute-done.7
  291.3 10.1 %fusion.8 = f32[512]{0:T(512)S(1)} fusion(f32[512,8192]{0,1:T(8,128)} %copy-done, f32[8192]{0:T(1024)S(1)} %bitcast.144, pred[512]{0:T(512)(128)(4,1)S(1)} %iota_compare_fusion.6, pred[8192]{0:T(1024)(128)(4,1)S(1)} %and.87), kind=kLoop, calls=%fused_computation.25 | loop fusion | flops 20971008 | bytes 16820736 | tf_op jit(solution)/shard_map/reduce_max | solution.py:115
  302.0 5.6 %exponential_reduce_fusion.1 = f32[512]{0:T(512)S(1)} fusion(f32[512,8192]{0,1:T(8,128)S(1)} %copy-done.1, f32[512]{0:T(512)S(1)} %fusion.8, f32[8192]{0:T(1024)S(1)} %bitcast.145, pred[512]{0:T(512)(128)(4,1)S(1)} %iota_compare_fusion.6, pred[8192]{0:T(1024)(128)(4,1)S(1)} %and.87), kind=kLoop, calls=%fused_computation.20 | loop fusion | flops 25165312 | bytes 16822784 | tf_op jit(solution)/shard_map/reduce_sum | solution.py:116
  307.7 4.8 %fusion.9 = f32[8192]{0:T(1024)S(1)} fusion(f32[512,8192]{0,1:T(8,128)S(1)} %copy-done.1, f32[512]{0:T(512)S(1)} %multiply_select_fusion, pred[512]{0:T(512)(128)(4,1)S(1)} %iota_compare_fusion.6, pred[8192]{0:T(1024)(128)(4,1)S(1)} %and.87), kind=kLoop, calls=%fused_computation.26 | loop fusion | flops 20963328 | bytes 16820736 | tf_op jit(solution)/shard_map/reduce_max | solution.py:122
  312.5 6.7 %exponential_reduce_fusion = f32[8192]{0:T(1024)S(1)} fusion(f32[512,8192]{0,1:T(8,128)S(1)} %copy-done.1, f32[8192]{0:T(1024)S(1)} %fusion.9, f32[512]{0:T(512)S(1)} %multiply_select_fusion, pred[512]{0:T(512)(128)(4,1)S(1)} %iota_compare_fusion.6, pred[8192]{0:T(1024)(128)(4,1)S(1)} %and.87), kind=kLoop, calls=%fused_computation.19 | loop fusion | flops 25157632 | bytes 16853504 | tf_op jit(solution)/shard_map/reduce_sum | solution.py:123
  319.2 25.1 %all_gather.19 = f32[8,2,8,512]{3,2,1,0:T(8,128)S(1)} all-gather(f32[1,2,8,512]{3,2,1,0:T(8,128)S(1)} %all_gather_reshape.15), channel_id=1, replica_groups=mesh['src'=4,'help'=8] {'help'}, dimensions={0}, use_global_device_ids=true | all-gather | bytes 294912 | tf_op jit(solution)/shard_map/all_gather | solution.py:30
  344.4 24.7 %all_gather.18 = f32[8,2,8,512]{3,2,1,0:T(8,128)S(1)} all-gather(f32[1,2,8,512]{3,2,1,0:T(8,128)S(1)} %all_gather_reshape.14), channel_id=1, replica_groups=mesh['src'=4,'help'=8] {'help'}, dimensions={0}, use_global_device_ids=true | all-gather | bytes 294912 | tf_op jit(solution)/shard_map/all_gather | solution.py:30
  369.5 11.8 %collective-permute-start.8 = (f32[8,512]{1,0:T(8,128)S(1)}, f32[8,512]{1,0:T(8,128)S(1)}, u32[]{:S(2)}, u32[]{:S(2)}) collective-permute-start(f32[8,512]{1,0:T(8,128)S(1)} %slice_bitcast_fusion.5), channel_id=1, source_target_pairs={{0,8},{8,16},{16,24},{24,0},{1,9},{9,17},{17,25},{25,1},{2,10},{10... | collective-permute-start | bytes 49160 | tf_op jit(solution)/shard_map/ppermute | solution.py:26
  382.5 2.1 collective-permute-start.10
  386.2 8.1 %convert_reduce_fusion = (f32[512]{0:T(512)S(1)}, bf16[512,8192]{0,1:T(8,128)(2,1)S(1)}) fusion(f32[512,8192]{0,1:T(8,128)} %copy-done, f32[8192]{0:T(1024)S(1)} %bitcast.146, f32[512]{0:T(512)S(1)} %multiply_select_fusion, pred[8192]{0:T(1024)(128)(4,1)S(1)} %and.87, pred[512]{0:T(512)(128)(4,1)S(1)} %iota_compare_fusion.6), kind=kLoop, calls=%fused_computation.18 | loop fusion | flops 33553920 | bytes 25211392 | tf_op jit(solution)/shard_map/reduce_sum | solution.py:139
  394.3 9.0 %fusion.12 = f32[512,512]{1,0:T(8,128)} fusion(bf16[512,8192]{0,1:T(8,128)(2,1)S(1)} %get-tuple-element.298, bf16[4096,512]{1,0:T(8,128)(2,1)} %collective-permute-done.4, bf16[4096,512]{1,0:T(8,128)(2,1)} %get-tuple-element.300, f32[512]{0:T(512)S(1)} %broadcast_select_fusion, pred[512]{0:T(512)(128)(4,1)S(1)} %iota_compare_fusion.6), kind=kOutput, calls=%fused_computation.33 | convolution fusion | flops 4312268800 | bytes 17828352 | tf_op jit(solution)/shard_map/dot_general | solution.py:138
  (100 shorter events, 10.7 us)
Async XLA Ops:
  0.6 16.0 %collective-permute-start.1 = (bf16[512,512]{1,0:T(8,128)(2,1)}, bf16[512,512]{1,0:T(8,128)(2,1)S(1)}, u32[]{:S(2)}, u32[]{:S(2)}) collective-permute-start(bf16[512,512]{1,0:T(8,128)(2,1)} %param.13), channel_id=1, source_target_pairs={{0,7},{1,0},{2,1},{3,2},{4,3},{5,4},{6,5},{7,6},{8,15},{9,8},{10,9... | collective-permute-start | bytes 1572872 | tf_op jit(solution)/shard_map/ppermute | solution.py:17
  16.7 24.5 %copy-start.3 = (bf16[512,512]{1,0:T(8,128)(2,1)}, bf16[512,512]{1,0:T(8,128)(2,1)S(1)}, u32[]{:S(2)}) copy-start(bf16[512,512]{1,0:T(8,128)(2,1)S(1)} %collective-permute-done.1) | copy-start | bytes 1572868
  18.0 23.2 %collective-permute-start.2 = (bf16[1024,512]{1,0:T(8,128)(2,1)S(1)}, bf16[1024,512]{1,0:T(8,128)(2,1)S(1)}, u32[]{:S(2)}, u32[]{:S(2)}) collective-permute-start(bf16[1024,512]{1,0:T(8,128)(2,1)S(1)} %pad_maximum_fusion.8), channel_id=1, source_target_pairs={{0,6},{1,7},{2,0},{3,1},{4,2},{5,3},{6,4},{7,5},{8,14},{9,15},{10,... | collective-permute-start | bytes 3145736 | tf_op jit(solution)/shard_map/ppermute | solution.py:17
  43.7 93.0 %collective-permute-start.3 = (bf16[2048,512]{1,0:T(8,128)(2,1)}, bf16[2048,512]{1,0:T(8,128)(2,1)S(1)}, u32[]{:S(2)}, u32[]{:S(2)}) collective-permute-start(bf16[2048,512]{1,0:T(8,128)(2,1)} %pad_maximum_fusion.3), channel_id=1, source_target_pairs={{0,4},{1,5},{2,6},{3,7},{4,0},{5,1},{6,2},{7,3},{8,12},{9,13},{10,... | collective-permute-start | bytes 6291464 | tf_op jit(solution)/shard_map/ppermute | solution.py:17
  43.9 93.0 %copy-start.2 = (bf16[512,512]{1,0:T(8,128)(2,1)S(1)}, bf16[512,512]{1,0:T(8,128)(2,1)}, u32[]{:S(2)}) copy-start(bf16[512,512]{1,0:T(8,128)(2,1)} %param.13) | copy-start | bytes 1572868
  43.9 93.1 %copy-start.4 = (bf16[512,512]{1,0:T(8,128)(2,1)S(1)}, bf16[512,512]{1,0:T(8,128)(2,1)}, u32[]{:S(2)}) copy-start(bf16[512,512]{1,0:T(8,128)(2,1)} %copy-done.3) | copy-start | bytes 1572868
  136.9 4.2 %copy-start.7 = (s32[1,2]{1,0:T(1,128)S(1)}, s32[1,2]{1,0:T(1,128)}, u32[]{:S(2)}) copy-start(s32[1,2]{1,0:T(1,128)} %param.11) | copy-start | bytes 28
  136.9 26.8 %copy-start.8 = (s32[2,64]{1,0:T(2,128)S(1)}, s32[2,64]{1,0:T(2,128)}, u32[]{:S(2)}) copy-start(s32[2,64]{1,0:T(2,128)} %param.9) | copy-start | bytes 1540
  136.9 26.8 %copy-start.9 = (s32[2,32]{1,0:T(2,128)S(1)}, s32[2,32]{1,0:T(2,128)}, u32[]{:S(2)}) copy-start(s32[2,32]{1,0:T(2,128)} %param.10) | copy-start | bytes 772
  137.1 54.9 %copy-start.5 = (bf16[512,512]{1,0:T(8,128)(2,1)S(1)}, bf16[512,512]{1,0:T(8,128)(2,1)}, u32[]{:S(2)}) copy-start(bf16[512,512]{1,0:T(8,128)(2,1)} %param.12) | copy-start | bytes 1572868
  140.0 48.9 %collective-permute-start.4 = (bf16[4096,512]{1,0:T(8,128)(2,1)}, bf16[4096,512]{1,0:T(8,128)(2,1)}, u32[]{:S(2)}, u32[]{:S(2)}) collective-permute-start(bf16[4096,512]{1,0:T(8,128)(2,1)} %get-tuple-element.300), channel_id=1, source_target_pairs={{0,24},{8,0},{16,8},{24,16},{1,25},{9,1},{17,9},{25,17},{2,26},{10... | collective-permute-start | bytes 12582920 | tf_op jit(solution)/shard_map/ppermute | solution.py:26
  158.8 30.0 %collective-permute-start = (s32[8,2]{0,1:T(2,128)S(1)}, s32[8,2]{0,1:T(2,128)S(1)}, u32[]{:S(2)}, u32[]{:S(2)}) collective-permute-start(s32[8,2]{0,1:T(2,128)S(1)} %bitcast.160), channel_id=1, source_target_pairs={{0,24},{8,0},{16,8},{24,16},{1,25},{9,1},{17,9},{25,17},{2,26},{10... | collective-permute-start | bytes 200 | tf_op jit(solution)/shard_map/ppermute | solution.py:26
  205.2 11.9 %copy-start = (f32[512,8192]{0,1:T(8,128)}, f32[512,8192]{0,1:T(8,128)S(1)}, u32[]{:S(2)}) copy-start(f32[512,8192]{0,1:T(8,128)S(1)} %get-tuple-element.306) | copy-start | bytes 50331652
  274.5 12.7 %collective-permute-start.5 = (f32[8,512]{1,0:T(8,128)S(1)}, f32[8,512]{1,0:T(8,128)S(1)}, u32[]{:S(2)}, u32[]{:S(2)}) collective-permute-start(f32[8,512]{1,0:T(8,128)S(1)} %slice_bitcast_fusion.7), channel_id=1, source_target_pairs={{0,8},{8,16},{16,24},{24,0},{1,9},{9,17},{17,25},{25,1},{2,10},{10... | collective-permute-start | bytes 49160 | tf_op jit(solution)/shard_map/ppermute | solution.py:26
  286.3 1.2 collective-permute-start.6
  287.5 3.8 collective-permute-start.7
  291.3 10.7 %copy-start.1 = (f32[512,8192]{0,1:T(8,128)S(1)}, f32[512,8192]{0,1:T(8,128)}, u32[]{:S(2)}) copy-start(f32[512,8192]{0,1:T(8,128)} %copy-done) | copy-start | bytes 50331652
  307.7 78.5 %copy-start.6 = (f32[512]{0:T(512)}, f32[512]{0:T(512)S(1)}, u32[]{:S(2)}) copy-start(f32[512]{0:T(512)S(1)} %multiply_select_fusion) | copy-start | bytes 6148
  369.5 12.7 %collective-permute-start.8 = (f32[8,512]{1,0:T(8,128)S(1)}, f32[8,512]{1,0:T(8,128)S(1)}, u32[]{:S(2)}, u32[]{:S(2)}) collective-permute-start(f32[8,512]{1,0:T(8,128)S(1)} %slice_bitcast_fusion.5), channel_id=1, source_target_pairs={{0,8},{8,16},{16,24},{24,0},{1,9},{9,17},{17,25},{25,1},{2,10},{10... | collective-permute-start | bytes 49160 | tf_op jit(solution)/shard_map/ppermute | solution.py:26
  381.3 1.2 collective-permute-start.9
  382.5 3.6 collective-permute-start.10
